TPU v7x, 32 devices: a whole 2x2x4 slice. The times are simulated.
32 devices in a mesh: expert: 16 (over z, x, core), tensor: 2 (over y).
Axes of the slice: x: 2, y: 2, z: 4, core: 2. Of those that a mesh axis runs over, the one named last changes fastest.
Arguments:
- query: bfloat16 [128, 8192], P(('expert', 'tensor')), may hold values from -6 to 6
- cache_keys: bfloat16 [128, 128, 4, 128], P(('expert', 'tensor')), may hold values from -6 to 6
- cache_values: bfloat16 [128, 128, 4, 128], P(('expert', 'tensor')), may hold values from -6 to 6
- lengths: int32 [128], P(('expert', 'tensor')), may hold values from 2 to 128, as said below
- residual: bfloat16 [128, 4096], P('tensor', 'expert'), may hold values from -12 to 12
- out_proj: bfloat16 [4096, 8192], P('expert', 'tensor'), may hold values from -0.0625 to 0.0625
- norm_gain: bfloat16 [4096], P('expert'), may hold values from 0.099609375 to 1.8984375
- expert_ids: int32 [128, 8], replicated, may hold values from 0 to 15, all different within a row; in each aligned block of 128 rows (0 to 127, 128 to 255, ...) at most 128 rows name the same one
- gate_scores: bfloat16 [128, 8], replicated, may hold values from 0.019897461 to 1
- w_gate: bfloat16 [16, 1536, 4096], P('expert', 'tensor'), may hold values from -0.09375 to 0.09375
- w_up: bfloat16 [16, 1536, 4096], P('expert', 'tensor'), may hold values from -0.09375 to 0.09375
- w_down: bfloat16 [16, 1536, 4096], P('expert', 'tensor'), may hold values from -0.15625 to 0.15625
Outputs:
- attn_residual: bfloat16 [128, 4096], P('tensor', 'expert')
- expert_mix: bfloat16 [128, 4096], P('tensor', 'expert')
Inputs may be any that keep to these rules, and one draw needn't show every extreme that they name: `expert_ids`: each row names 8 different experts; no expert is named by more than 128 rows, and one by exactly 128. `lengths`: some row has exactly 128.
All inputs are finite; a program needn't handle non-finite values.
Results may differ from a plain program's by a relative error of at most 0.018.
Values may be sent and summed in bfloat16 or wider, within the bound.
A program may use at most 64 MiB of HBM per device.

v0:
```python
import jax
import jax.numpy as jnp
from jax import lax
from jax.sharding import PartitionSpec as P

floor_value = -1e30
epsilon = 1e-06


def softmax_parts(queries, key_block, value_block, usable, score_scale):
    scores = (
        jnp.einsum("rkgd,rpkd->rkgp", queries, key_block, preferred_element_type=jnp.float32)
        * score_scale
    )
    usable_mask = usable[:, None, None, :]
    peak = jnp.max(jnp.where(usable_mask, scores, floor_value), axis=-1)
    raw_weights = jnp.where(usable_mask, jnp.exp(scores - peak[..., None]), 0.0)
    weight_sum = jnp.sum(raw_weights, axis=-1)
    weighted = jnp.einsum("rkgp,rpkd->rkgd", raw_weights, value_block.astype(jnp.float32))
    return (weight_sum, weighted)


def body(
    query,
    cache_keys,
    cache_values,
    lengths,
    residual,
    out_proj,
    norm_gain,
    expert_ids,
    gate_scores,
    w_gate,
    w_up,
    w_down,
):
    row_count, full_heads_width = query.shape
    cache_len = cache_keys.shape[1]
    kv_count = cache_keys.shape[2]
    head_size = cache_keys.shape[3]
    head_count = full_heads_width // head_size
    group_size = head_count // kv_count
    score_scale = head_size ** (-0.5)
    usable = jnp.arange(cache_len, dtype=jnp.int32)[None, :] < lengths[:, None]
    grouped = query.reshape(row_count, kv_count, group_size, head_size)
    weight_sum, weighted = softmax_parts(grouped, cache_keys, cache_values, usable, score_scale)
    context_rows_own = (
        (weighted / weight_sum[..., None]).astype(jnp.bfloat16).reshape(row_count, full_heads_width)
    )
    context = lax.all_to_all(context_rows_own, "tensor", split_axis=1, concat_axis=0, tiled=True)
    attn_part = jnp.dot(
        lax.all_gather(context, "expert", axis=0, tiled=True),
        out_proj.T,
        preferred_element_type=jnp.float32,
    )
    attn_share = lax.psum_scatter(attn_part, "tensor", scatter_dimension=0, tiled=True)
    hidden_state = residual.astype(jnp.float32) + attn_share
    squares = lax.psum(jnp.sum(hidden_state * hidden_state, axis=1), "expert")
    full_width = hidden_state.shape[1] * lax.axis_size("expert")
    scaled_share = (hidden_state * norm_gain.astype(jnp.float32)[None, :]).astype(jnp.bfloat16)
    scaled = lax.all_gather(
        lax.all_gather(scaled_share, "tensor", axis=0, tiled=True), "expert", axis=1, tiled=True
    )
    mean_all = lax.all_gather(squares / full_width, "tensor", axis=0, tiled=True)
    row_scale = lax.rsqrt(mean_all + epsilon)[:, None]
    experts_local = w_gate.shape[0]
    gate_weight = gate_scores.astype(jnp.float32)
    gate_weight = gate_weight / jnp.sum(gate_weight, axis=1, keepdims=True)
    mixed = None
    for local in range(experts_local):
        expert = lax.axis_index("expert") * experts_local + local
        weight = jnp.sum(jnp.where(expert_ids == expert, gate_weight, 0.0), axis=1, keepdims=True)
        gate_proj = row_scale * lax.dot_general(
            scaled, w_gate[local], (((1,), (1,)), ((), ())), preferred_element_type=jnp.float32
        )
        up_proj = row_scale * lax.dot_general(
            scaled, w_up[local], (((1,), (1,)), ((), ())), preferred_element_type=jnp.float32
        )
        activation = (jax.nn.silu(gate_proj) * up_proj).astype(jnp.bfloat16)
        part = weight * jnp.dot(activation, w_down[local], preferred_element_type=jnp.float32)
        mixed = part if mixed is None else mixed + part
    mixed = lax.psum_scatter(mixed.astype(jnp.bfloat16), "tensor", scatter_dimension=0, tiled=True)
    mixed_share = lax.psum_scatter(mixed, "expert", scatter_dimension=1, tiled=True)
    return (hidden_state.astype(jnp.bfloat16), mixed_share)


def solution(mesh):
    in_specs = (
        P(("expert", "tensor"), None),
        P(("expert", "tensor"), None, None, None),
        P(("expert", "tensor"), None, None, None),
        P(("expert", "tensor")),
        P("tensor", "expert"),
        P("expert", "tensor"),
        P("expert"),
        P(),
        P(),
        P("expert", "tensor", None),
        P("expert", "tensor", None),
        P("expert", "tensor", None),
    )
    out_specs = (P("tensor", "expert"), P("tensor", "expert"))
    return jax.shard_map(body, mesh=mesh, in_specs=in_specs, out_specs=out_specs, check_vma=False)
```

profile of v0, /device:TPU:0, one launch (start us, length us, event | category | flops | bytes accessed | tf_op | source)
XLA Modules:
  0.0 218.9 jit_solution(551768819832569103)
XLA Ops:
  7.3 0.9 iota_compare_fusion
  8.1 0.8 copy.19
  9.0 1.5 select_reduce_fusion
  10.5 2.5 %fusion = f32[4,4,16,128]{3,2,1,0:T(8,128)S(1)} fusion(f32[4,4,16,128]{3,2,1,0:T(8,128)S(1)} %get-tuple-element.6, f32[4,4,16]{2,1,0:T(4,128)S(1)} %get-tuple-element.5, pred[4,128]{1,0:T(4,128)(4,1)S(1)} %iota_compare_fusion), kind=kOutput, calls=%fused_computation | output fusion | flops 65919 | bytes 263680 | tf_op jit(solution)/shard_map/div | solution.py:48
  13.0 1.4 fusion.25
  14.4 0.1 copy.18
  14.5 8.2 %all_to_all.19 = bf16[4,2,4096]{2,0,1:T(4,128)(2,1)S(1)} all-to-all(bf16[4,2,4096]{2,0,1:T(4,128)(2,1)S(1)} %copy.18), channel_id=1, replica_groups=mesh['expert'=16,'tensor'=2] {'tensor'}, dimensions={1} | all-to-all | bytes 131072 | tf_op jit(solution)/shard_map/all_to_all | solution.py:50
  22.7 0.6 all_to_all.17
  23.3 0.0 reduce-scatter.4.cloned.1.call-start
  23.4 38.2 %all-gather.3.cloned.1.call-done = bf16[128,4096]{1,0:T(8,128)(2,1)} async-done(((bf16[8,4096]{1,0:T(8,128)(2,1)}), bf16[128,4096]{1,0:T(8,128)(2,1)}) %all-gather.3.cloned.1.call-update) | async-done | bytes 1048592 | tf_op jit(solution)/shard_map/all_gather | solution.py:52
  61.6 2.7 %fusion.50 = f32[128,256]{1,0:T(8,128)} fusion(bf16[128,4096]{1,0:T(8,128)(2,1)} %all-gather.3.cloned.1.call-done, bf16[256,4096]{1,0:T(8,128)(2,1)S(1)} %copy-done), kind=kOutput, calls=%fused_computation.48 | convolution fusion | flops 268435456 | bytes 3276800 | tf_op jit(solution)/shard_map/dot_general | solution.py:51
  64.3 0.0 all-gather.5.cloned.1.call-start
  64.4 9.4 %reduce-scatter.4.cloned.1.call-done = f32[64,256]{1,0:T(8,128)} async-done(((f32[128,256]{1,0:T(8,128)}), f32[64,256]{1,0:T(8,128)}) %reduce-scatter.4.cloned.1.call-update) | async-done | bytes 65552 | tf_op jit(solution)/shard_map/reduce_scatter | solution.py:56
  73.8 1.6 multiply_reduce_fusion
  75.4 4.7 %all_gather.14 = bf16[128,256]{1,0:T(8,128)(2,1)} all-gather(bf16[64,256]{1,0:T(8,128)(2,1)S(1)} %get-tuple-element.3), channel_id=1, replica_groups=mesh['expert'=16,'tensor'=2] {'tensor'}, dimensions={0}, use_global_device_ids=true | all-gather | bytes 98304 | tf_op jit(solution)/shard_map/all_gather | solution.py:62
  80.1 0.0 reduce-scatter.6.cloned.1.call-start
  80.2 0.6 dynamic-slice
  81.5 31.9 %psum.7 = f32[64]{0:T(128)S(1)} all-reduce(f32[64]{0:T(128)S(1)} %get-tuple-element.2), channel_id=1, replica_groups=mesh['expert'=16,'tensor'=2] {'expert'}, use_global_device_ids=true, to_apply=%region_6.7 | all-reduce | flops 64 | bytes 512 | tf_op jit(solution)/shard_map/psum | solution.py:58
  113.4 0.1 multiply_dynamic-update-slice_fusion
  113.5 4.9 %all-reduce = f32[128]{0:T(128)S(1)} all-reduce(f32[128]{0:T(128)S(1)} %multiply_dynamic-update-slice_fusion), channel_id=1, replica_groups=mesh['expert'=16,'tensor'=2] {'tensor'}, use_global_device_ids=true, to_apply=%add | all-reduce | flops 128 | bytes 1024
  118.5 5.4 %fusion.13 = f32[128,768]{1,0:T(8,128)S(1)} fusion(bf16[128,4096]{1,0:T(8,128)(2,1)} %all-gather.5.cloned.1.call-done, bf16[1,768,4096]{2,1,0:T(8,128)(2,1)} %param.21, f32[128]{0:T(128)S(1)} %add_rsqrt_fusion), kind=kOutput, calls=%fused_computation.9 | convolution fusion | flops 805404672 | bytes 7733760 | tf_op jit(solution)/shard_map/dot_general | solution.py:73
  123.9 9.7 %fusion.10 = bf16[128,4096]{1,0:T(8,128)(2,1)} fusion(bf16[1,768,4096]{2,1,0:T(8,128)(2,1)} %param.23, f32[128]{0:T(128)S(1)} %fusion.46, bf16[128,4096]{1,0:T(8,128)(2,1)S(1)} %copy-done.1, bf16[1,768,4096]{2,1,0:T(8,128)(2,1)} %param.22, f32[128,768]{1,0:T(8,128)S(1)} %fusion.13, f32[128]{0:T(128)S(1)} %add_rsqrt_fusion), kind=kOutput, calls=%fused_computation.8 | convolution fusion | flops 1612349440 | bytes 15074304 | tf_op jit(solution)/shard_map/dot_general | solution.py:80
  133.6 18.6 %reduce-scatter.6.cloned.1.call-done = bf16[64,4096]{1,0:T(8,128)(2,1)} async-done(((bf16[128,4096]{1,0:T(8,128)(2,1)}), bf16[64,4096]{1,0:T(8,128)(2,1)}) %reduce-scatter.6.cloned.1.call-update) | async-done | bytes 524304 | tf_op jit(solution)/shard_map/reduce_scatter | solution.py:82
  152.2 60.1 %reduce-scatter.8.cloned.1.call-done = bf16[64,256]{1,0:T(8,128)(2,1)} async-done(((bf16[64,4096]{1,0:T(8,128)(2,1)}), bf16[64,256]{1,0:T(8,128)(2,1)}) %reduce-scatter.8.cloned.1.call-update) | async-done | bytes 32784 | tf_op jit(solution)/shard_map/reduce_scatter | solution.py:83
  (28 shorter events, 0.3 us)
Async XLA Ops:
  7.2 54.4 %copy-start = (bf16[256,4096]{1,0:T(8,128)(2,1)S(1)}, bf16[256,4096]{1,0:T(8,128)(2,1)}, u32[]{:S(2)}) copy-start(bf16[256,4096]{1,0:T(8,128)(2,1)} %param.17) | copy-start | bytes 6291460
  7.2 73.0 %copy-start.6 = (u32[32]{0:T(128)S(1)}, u32[32]{0:T(128)}, u32[]{:S(2)}) copy-start(u32[32]{0:T(128)} %constant.31) | copy-start | bytes 388
  7.2 57.2 %copy-start.5 = (bf16[256]{0:T(256)(128)(2,1)S(1)}, bf16[256]{0:T(256)(128)(2,1)}, u32[]{:S(2)}) copy-start(bf16[256]{0:T(256)(128)(2,1)} %param.18) | copy-start | bytes 1540
  7.2 66.6 %copy-start.2 = (bf16[64,256]{1,0:T(8,128)(2,1)S(1)}, bf16[64,256]{1,0:T(8,128)(2,1)}, u32[]{:S(2)}) copy-start(bf16[64,256]{1,0:T(8,128)(2,1)} %param.16) | copy-start | bytes 98308
  7.2 74.2 %copy-start.3 = (bf16[128,8]{0,1:T(8,128)(2,1)S(1)}, bf16[128,8]{0,1:T(8,128)(2,1)}, u32[]{:S(2)}) copy-start(bf16[128,8]{0,1:T(8,128)(2,1)} %param.20) | copy-start | bytes 6148
  7.2 74.2 %copy-start.4 = (s32[128,8]{0,1:T(8,128)S(1)}, s32[128,8]{0,1:T(8,128)}, u32[]{:S(2)}) copy-start(s32[128,8]{0,1:T(8,128)} %param.19) | copy-start | bytes 12292
  7.2 54.4 %all-gather.3.cloned.1.call-start = ((), (), s32[]{:S(2)}) async-start(), calls=%async_computation.4 | async-start | bytes 1114112 | tf_op jit(solution)/shard_map/all_gather | solution.py:52
  23.3 50.5 %reduce-scatter.4.cloned.1.call-start = ((), (), s32[]{:S(2)}) async-start(), calls=%async_computation.5 | async-start | bytes 196608 | tf_op jit(solution)/shard_map/reduce_scatter | solution.py:56
  64.3 54.1 %all-gather.5.cloned.1.call-start = ((), (), s32[]{:S(2)}) async-start(), calls=%async_computation.6 | async-start | bytes 1114112 | tf_op jit(solution)/shard_map/all_gather | solution.py:61
  80.1 72.1 %reduce-scatter.6.cloned.1.call-start = ((), (), s32[]{:S(2)}) async-start(), calls=%async_computation.7 | async-start | bytes 1572864 | tf_op jit(solution)/shard_map/reduce_scatter | solution.py:82
  118.5 5.4 %copy-start.1 = (bf16[128,4096]{1,0:T(8,128)(2,1)S(1)}, bf16[128,4096]{1,0:T(8,128)(2,1)}, u32[]{:S(2)}) copy-start(bf16[128,4096]{1,0:T(8,128)(2,1)} %all-gather.5.cloned.1.call-done) | copy-start | bytes 3145732
  133.6 78.8 %reduce-scatter.8.cloned.1.call-start = ((), (), s32[]{:S(2)}) async-start(), calls=%async_computation.8 | async-start | bytes 557056 | tf_op jit(solution)/shard_map/reduce_scatter | solution.py:83
Sparse Core Ops, SparseCore 0:
  23.4 38.1 all-gather.2
  64.5 9.3 reduce-scatter.3
  80.3 36.6 all-gather.4
  133.7 18.4 reduce-scatter.5
  156.2 56.1 reduce-scatter.7
where the time goes:
time: 219 us
  waiting for transfers between devices  126 us (58%)
  blocking collectives  49.7 us (23%)
  matrix products  20.7 us (9%)
  between operations  14.6 us (7%)
  other arithmetic  5.06 us (2%)
  local copies, waits for them, and re-layouts  2.19 us (1%)
    reduce_scatter x1, waiting for transfers between devices, body(): lax.psum_scatter(mixed, 'expert', scatter_dimension=1, tiled=True)  60.1 us
    all_gather x1, waiting for transfers between devices, body(): lax.all_gather(context, 'expert', axis=0, tiled=True)  38.2 us
    psum x1, blocking collectives, body(): squares = lax.psum(jnp.sum(hidden_state * hidden_state, axis=1), 'expert')  31.9 us
    reduce_scatter x1, waiting for transfers between devices, body(): lax.psum_scatter(mixed.astype(jnp.bfloat16), 'tensor', scatter_dimension=...  18.6 us
    dot_general x1, matrix products, body(): jnp.dot(activation, w_down[local], preferred_element_type=jnp.float32)  9.66 us
    reduce_scatter x1, waiting for transfers between devices, body(): lax.psum_scatter(attn_part, 'tensor', scatter_dimension=0, tiled=True)  9.44 us
    all_to_all x1, blocking collectives, body(): lax.all_to_all(context_rows_own, 'tensor', split_axis=1, concat_axis=0, t...  8.18 us
    dot_general x1, matrix products, body(): lax.dot_general(scaled, w_gate[local], (((1,), (1,)), ((), ())), preferre...  5.4 us
  transfers between devices with their start and end apart: 5, of which 4 were waited for; matrix products, arithmetic and copies ran while one was open for 0% of the time, Pallas kernels for 0%

commit v1 on v0

--- a/solution.py
+++ b/solution.py
@@ -5,6 +5,11 @@
 
 floor_value = -1e30
 epsilon = 1e-06
+
+
+def all_by_exchange(shard, name, dim):
+    outgoing = jnp.stack([shard] * lax.axis_size(name))
+    return jnp.concatenate(lax.all_to_all(outgoing, name, 0, 0), axis=dim)
 
 
 def softmax_parts(queries, key_block, value_block, usable, score_scale):
@@ -49,9 +54,7 @@
     )
     context = lax.all_to_all(context_rows_own, "tensor", split_axis=1, concat_axis=0, tiled=True)
     attn_part = jnp.dot(
-        lax.all_gather(context, "expert", axis=0, tiled=True),
-        out_proj.T,
-        preferred_element_type=jnp.float32,
+        all_by_exchange(context, "expert", 0), out_proj.T, preferred_element_type=jnp.float32
     )
     attn_share = lax.psum_scatter(attn_part, "tensor", scatter_dimension=0, tiled=True)
     hidden_state = residual.astype(jnp.float32) + attn_share

time: 219 us -> 210 us (0.959)
  waiting for transfers between devices: 126 us -> 88.7 us
  blocking collectives: 49.7 us -> 80.1 us
    all_gather x1 -> x0, waiting for transfers between devices: 38.2 us -> none  [body(): lax.all_gather(context, 'expert', axis=0, tiled=True)]
    all_to_all x0 -> x1, blocking collectives: none -> 30.4 us  [all_by_exchange(): return jnp.concatenate(lax.all_to_all(outgoing, name, 0, 0), axis=dim)]
  transfers between devices with their start and end apart: 5 -> 4, of which waited for: 4 -> 3; matrix products, arithmetic and copies ran while one was open for 0% -> 0% of each run, Pallas kernels for 0% -> 0%
where the time goes in v1:
time: 210 us
  waiting for transfers between devices  88.7 us (42%)
  blocking collectives  80.1 us (38%)
  matrix products  19.4 us (9%)
  between operations  14.6 us (7%)
  other arithmetic  5.06 us (2%)
    reduce_scatter x1, waiting for transfers between devices, body(): lax.psum_scatter(mixed, 'expert', scatter_dimension=1, tiled=True)  60.2 us
    psum x1, blocking collectives, body(): squares = lax.psum(jnp.sum(hidden_state * hidden_state, axis=1), 'expert')  31.9 us
    all_to_all x1, blocking collectives, all_by_exchange(): return jnp.concatenate(lax.all_to_all(outgoing, name, 0, 0), axis=dim)  30.4 us
    reduce_scatter x1, waiting for transfers between devices, body(): lax.psum_scatter(mixed.astype(jnp.bfloat16), 'tensor', scatter_dimension=...  18.6 us
    reduce_scatter x1, waiting for transfers between devices, body(): lax.psum_scatter(attn_part, 'tensor', scatter_dimension=0, tiled=True)  9.92 us
    dot_general x1, matrix products, body(): jnp.dot(activation, w_down[local], preferred_element_type=jnp.float32)  9.67 us
    all_to_all x1, blocking collectives, body(): lax.all_to_all(context_rows_own, 'tensor', split_axis=1, concat_axis=0, t...  8.18 us
    dot_general x1, matrix products, body(): lax.dot_general(scaled, w_gate[local], (((1,), (1,)), ((), ())), preferre...  5.4 us
  transfers between devices with their start and end apart: 4, of which 3 were waited for; matrix products, arithmetic and copies ran while one was open for 0% of the time, Pallas kernels for 0%

profile of v1, /device:TPU:0, one launch (start us, length us, event | category | flops | bytes accessed | tf_op | source)
XLA Modules:
  0.0 209.7 jit_solution(3295761533697509364)
XLA Ops:
  7.3 0.9 iota_compare_fusion
  8.1 0.8 copy.19
  9.0 1.5 select_reduce_fusion
  10.5 2.5 %fusion = f32[4,4,16,128]{3,2,1,0:T(8,128)S(1)} fusion(f32[4,4,16,128]{3,2,1,0:T(8,128)S(1)} %get-tuple-element.6, f32[4,4,16]{2,1,0:T(4,128)S(1)} %get-tuple-element.5, pred[4,128]{1,0:T(4,128)(4,1)S(1)} %iota_compare_fusion), kind=kOutput, calls=%fused_computation | output fusion | flops 65919 | bytes 263680 | tf_op jit(solution)/shard_map/div | solution.py:53
  13.0 1.4 fusion.25
  14.4 0.1 copy.18
  14.5 8.2 %all_to_all.21 = bf16[4,2,4096]{2,0,1:T(4,128)(2,1)S(1)} all-to-all(bf16[4,2,4096]{2,0,1:T(4,128)(2,1)S(1)} %copy.18), channel_id=1, replica_groups=mesh['expert'=16,'tensor'=2] {'tensor'}, dimensions={1} | all-to-all | bytes 131072 | tf_op jit(solution)/shard_map/all_to_all | solution.py:55
  22.7 0.1 stack.5
  22.8 30.4 %all_to_all.22 = bf16[16,8,4096]{2,1,0:T(8,128)(2,1)S(1)} all-to-all(bf16[16,8,4096]{2,1,0:T(8,128)(2,1)S(1)} %stack.5), channel_id=1, replica_groups=mesh['expert'=16,'tensor'=2] {'expert'}, dimensions={0} | all-to-all | bytes 2097152 | tf_op jit(solution)/shard_map/all_to_all | solution.py:12
  53.2 1.5 fusion.26
  54.7 0.0 all-gather.2.cloned.1.call-start
  54.7 9.9 %reduce-scatter.4.cloned.1.call-done = f32[64,256]{1,0:T(8,128)} async-done(((f32[128,256]{1,0:T(8,128)}), f32[64,256]{1,0:T(8,128)}) %reduce-scatter.4.cloned.1.call-update) | async-done | bytes 65552 | tf_op jit(solution)/shard_map/reduce_scatter | solution.py:59
  64.7 1.6 multiply_reduce_fusion
  66.2 4.7 %all_gather.10 = bf16[128,256]{1,0:T(8,128)(2,1)} all-gather(bf16[64,256]{1,0:T(8,128)(2,1)S(1)} %get-tuple-element.3), channel_id=1, replica_groups=mesh['expert'=16,'tensor'=2] {'tensor'}, dimensions={0}, use_global_device_ids=true | all-gather | bytes 98304 | tf_op jit(solution)/shard_map/all_gather | solution.py:65
  71.0 0.0 reduce-scatter.6.cloned.1.call-start
  71.0 0.6 dynamic-slice
  72.3 31.9 %psum.7 = f32[64]{0:T(128)S(1)} all-reduce(f32[64]{0:T(128)S(1)} %get-tuple-element.2), channel_id=1, replica_groups=mesh['expert'=16,'tensor'=2] {'expert'}, use_global_device_ids=true, to_apply=%region_6.7 | all-reduce | flops 64 | bytes 512 | tf_op jit(solution)/shard_map/psum | solution.py:61
  104.3 0.1 multiply_dynamic-update-slice_fusion
  104.3 4.9 %all-reduce = f32[128]{0:T(128)S(1)} all-reduce(f32[128]{0:T(128)S(1)} %multiply_dynamic-update-slice_fusion), channel_id=1, replica_groups=mesh['expert'=16,'tensor'=2] {'tensor'}, use_global_device_ids=true, to_apply=%add | all-reduce | flops 128 | bytes 1024
  109.3 5.4 %fusion.13 = f32[128,768]{1,0:T(8,128)S(1)} fusion(bf16[128,4096]{1,0:T(8,128)(2,1)} %all-gather.2.cloned.1.call-done, bf16[1,768,4096]{2,1,0:T(8,128)(2,1)} %param.21, f32[128]{0:T(128)S(1)} %add_rsqrt_fusion), kind=kOutput, calls=%fused_computation.9 | convolution fusion | flops 805404672 | bytes 7733760 | tf_op jit(solution)/shard_map/dot_general | solution.py:76
  114.7 9.7 %fusion.10 = bf16[128,4096]{1,0:T(8,128)(2,1)} fusion(bf16[1,768,4096]{2,1,0:T(8,128)(2,1)} %param.23, f32[128]{0:T(128)S(1)} %fusion.48, bf16[128,4096]{1,0:T(8,128)(2,1)S(1)} %copy-done.1, bf16[1,768,4096]{2,1,0:T(8,128)(2,1)} %param.22, f32[128,768]{1,0:T(8,128)S(1)} %fusion.13, f32[128]{0:T(128)S(1)} %add_rsqrt_fusion), kind=kOutput, calls=%fused_computation.8 | convolution fusion | flops 1612349440 | bytes 15074304 | tf_op jit(solution)/shard_map/dot_general | solution.py:83
  124.4 0.0 reduce-scatter.8.cloned.1.call-start
  124.4 18.6 %reduce-scatter.6.cloned.1.call-done = bf16[64,4096]{1,0:T(8,128)(2,1)} async-done(((bf16[128,4096]{1,0:T(8,128)(2,1)}), bf16[64,4096]{1,0:T(8,128)(2,1)}) %reduce-scatter.6.cloned.1.call-update) | async-done | bytes 524304 | tf_op jit(solution)/shard_map/reduce_scatter | solution.py:85
  143.0 60.2 %reduce-scatter.8.cloned.1.call-done = bf16[64,256]{1,0:T(8,128)(2,1)} async-done(((bf16[64,4096]{1,0:T(8,128)(2,1)}), bf16[64,256]{1,0:T(8,128)(2,1)}) %reduce-scatter.8.cloned.1.call-update) | async-done | bytes 32784 | tf_op jit(solution)/shard_map/reduce_scatter | solution.py:86
  (27 shorter events, 0.3 us)
Async XLA Ops:
  7.2 46.0 %copy-start = (bf16[256,4096]{1,0:T(8,128)(2,1)S(1)}, bf16[256,4096]{1,0:T(8,128)(2,1)}, u32[]{:S(2)}) copy-start(bf16[256,4096]{1,0:T(8,128)(2,1)} %param.17) | copy-start | bytes 6291460
  7.2 63.8 %copy-start.6 = (u32[32]{0:T(128)S(1)}, u32[32]{0:T(128)}, u32[]{:S(2)}) copy-start(u32[32]{0:T(128)} %constant.31) | copy-start | bytes 388
  7.2 47.5 %copy-start.5 = (bf16[256]{0:T(256)(128)(2,1)S(1)}, bf16[256]{0:T(256)(128)(2,1)}, u32[]{:S(2)}) copy-start(bf16[256]{0:T(256)(128)(2,1)} %param.18) | copy-start | bytes 1540
  7.2 57.5 %copy-start.2 = (bf16[64,256]{1,0:T(8,128)(2,1)S(1)}, bf16[64,256]{1,0:T(8,128)(2,1)}, u32[]{:S(2)}) copy-start(bf16[64,256]{1,0:T(8,128)(2,1)} %param.16) | copy-start | bytes 98308
  7.2 65.0 %copy-start.3 = (bf16[128,8]{0,1:T(8,128)(2,1)S(1)}, bf16[128,8]{0,1:T(8,128)(2,1)}, u32[]{:S(2)}) copy-start(bf16[128,8]{0,1:T(8,128)(2,1)} %param.20) | copy-start | bytes 6148
  7.2 65.1 %copy-start.4 = (s32[128,8]{0,1:T(8,128)S(1)}, s32[128,8]{0,1:T(8,128)}, u32[]{:S(2)}) copy-start(s32[128,8]{0,1:T(8,128)} %param.19) | copy-start | bytes 12292
  7.2 57.4 %reduce-scatter.4.cloned.1.call-start = ((), (), s32[]{:S(2)}) async-start(), calls=%async_computation.5 | async-start | bytes 196608 | tf_op jit(solution)/shard_map/reduce_scatter | solution.py:59
  54.7 54.6 %all-gather.2.cloned.1.call-start = ((), (), s32[]{:S(2)}) async-start(), calls=%async_computation.6 | async-start | bytes 1114112 | tf_op jit(solution)/shard_map/all_gather | solution.py:64
  71.0 72.1 %reduce-scatter.6.cloned.1.call-start = ((), (), s32[]{:S(2)}) async-start(), calls=%async_computation.7 | async-start | bytes 1572864 | tf_op jit(solution)/shard_map/reduce_scatter | solution.py:85
  109.3 5.4 %copy-start.1 = (bf16[128,4096]{1,0:T(8,128)(2,1)S(1)}, bf16[128,4096]{1,0:T(8,128)(2,1)}, u32[]{:S(2)}) copy-start(bf16[128,4096]{1,0:T(8,128)(2,1)} %all-gather.2.cloned.1.call-done) | copy-start | bytes 3145732
  124.4 78.8 %reduce-scatter.8.cloned.1.call-start = ((), (), s32[]{:S(2)}) async-start(), calls=%async_computation.8 | async-start | bytes 557056 | tf_op jit(solution)/shard_map/reduce_scatter | solution.py:86
Sparse Core Ops, SparseCore 0:
  54.8 9.8 reduce-scatter.3
  71.1 36.6 all-gather.1
  124.5 18.4 reduce-scatter.5
  147.0 56.1 reduce-scatter.7
